TPU v7x, 32 devices: a whole 2x2x4 slice. The times are simulated.
32 devices in a mesh: view: 4 (over z), cell: 8 (over y, x, core).
Axes of the slice: x: 2, y: 2, z: 4, core: 2. Of those that a mesh axis runs over, the one named last changes fastest.
Arguments:
- params: float32 [59, 65536], P(None, 'cell'), may hold values from -6.22 to 3.2, as said below
- camera: float32 [4, 11], P('view'), may hold values from -0.3 to 1536, as said below
- targets: float32 [4, 256, 3, 256], P('view', 'cell'), may hold values from 0 to 1
- send_blocks: int32 [4, 8, 8, 16], P('view', 'cell'), may hold values from 0 to 255, as said below
- tile_blocks: int32 [4, 256, 16], P('view', 'cell'), may hold values from -1 to 127, as said below
- tile_order: int32 [4, 256, 512], P('view', 'cell'), may hold values from 0 to 511, as said below
Outputs:
- image: float32 [4, 256, 3, 256], P('view', 'cell')
- grads: float32 [59, 65536], P(None, 'cell')
Inputs may be any that keep to these rules, and one draw needn't show every extreme that they name: `params`: rows 0 to 2 lie in -3.2 to 3.2, rows 3 to 5 in log 0.002 to log 0.025, row 6 in 1 to 2, rows 7 to 9 in -1 to 1, row 10 in -3 to 2, rows 11 to 58 in -1.5 to 1.5. `camera`: quaternion first entry 1 to 2, its others -0.15 to 0.15, first two translation entries -0.3 to 0.3, third translation entry 4.5 to 6, focal lengths 2 to 3 times 16 max(32, 256 div 32), principal point within 20 of the image centre. `send_blocks`: the 16 numbers for one view, owner and receiving device are distinct. `tile_blocks`: A tile's live entries are distinct and come first, -1 fills the rest, and every tile has at least one live entry. `tile_order`: each tile's row is a permutation of 0 to 511.
All inputs are finite; a program needn't handle non-finite values.
Results may differ from a plain program's by a relative error of at most 0.0003.
Values sent between devices are 32-bit elements; how exact they have to be, the bound alone decides.
A program may use at most 128 MiB of HBM per device.

v0:
```python
import math
import jax
import jax.numpy as jnp
from jax import lax
from jax.sharding import PartitionSpec as P

BLOCK_GAUSSIANS = 32
TX = 32
HIGHEST_PRECISE = lax.Precision.HIGHEST
SH_ZERO = 0.28209479177387814
SH_ONE = 0.4886025119029199
SH_TWO = [
    1.0925484305920792,
    -1.0925484305920792,
    0.31539156525252005,
    -1.0925484305920792,
    0.5462742152960396,
]
SH_THREE = [
    -0.5900435899266435,
    2.890611442640554,
    -0.4570457994644658,
    0.3731763325901154,
    -0.4570457994644658,
    1.445305721320277,
    -0.5900435899266435,
]


def quat_matrix(qw, qx, qy, qz):
    return [
        [1.0 - 2.0 * (qy * qy + qz * qz), 2.0 * (qx * qy - qw * qz), 2.0 * (qx * qz + qw * qy)],
        [2.0 * (qx * qy + qw * qz), 1.0 - 2.0 * (qx * qx + qz * qz), 2.0 * (qy * qz - qw * qx)],
        [2.0 * (qx * qz - qw * qy), 2.0 * (qy * qz + qw * qx), 1.0 - 2.0 * (qx * qx + qy * qy)],
    ]


def sh_basis(dirx, diry, dirz):
    xx, yy, zz = (dirx * dirx, diry * diry, dirz * dirz)
    return [
        SH_ZERO + 0.0 * dirx,
        -SH_ONE * diry,
        SH_ONE * dirz,
        -SH_ONE * dirx,
        SH_TWO[0] * dirx * diry,
        SH_TWO[1] * diry * dirz,
        SH_TWO[2] * (2.0 * zz - xx - yy),
        SH_TWO[3] * dirx * dirz,
        SH_TWO[4] * (xx - yy),
        SH_THREE[0] * diry * (3.0 * xx - yy),
        SH_THREE[1] * dirx * diry * dirz,
        SH_THREE[2] * diry * (4.0 * zz - xx - yy),
        SH_THREE[3] * dirz * (2.0 * zz - 3.0 * xx - 3.0 * yy),
        SH_THREE[4] * dirx * (4.0 * zz - xx - yy),
        SH_THREE[5] * dirz * (xx - yy),
        SH_THREE[6] * dirx * (xx - 3.0 * yy),
    ]


def project(gauss, camera_row):
    cam_norm = jnp.sqrt(jnp.sum(camera_row[0:4] * camera_row[0:4]))
    cam_quat = camera_row[0:4] / cam_norm
    rotation = quat_matrix(cam_quat[0], cam_quat[1], cam_quat[2], cam_quat[3])
    focal_x, focal_y, centre_x, centre_y = (
        camera_row[7],
        camera_row[8],
        camera_row[9],
        camera_row[10],
    )
    cam_pos = [
        rotation[i][0] * gauss[0]
        + rotation[i][1] * gauss[1]
        + rotation[i][2] * gauss[2]
        + camera_row[4 + i]
        for i in range(3)
    ]
    inverse = 1.0 / cam_pos[2]
    screen_u = focal_x * cam_pos[0] * inverse + centre_x
    screen_w = focal_y * cam_pos[1] * inverse + centre_y
    gauss_norm = jnp.sqrt(
        gauss[6] * gauss[6] + gauss[7] * gauss[7] + gauss[8] * gauss[8] + gauss[9] * gauss[9]
    )
    grot = quat_matrix(
        gauss[6] / gauss_norm, gauss[7] / gauss_norm, gauss[8] / gauss_norm, gauss[9] / gauss_norm
    )
    scales = [jnp.exp(gauss[3 + k]) for k in range(3)]
    axes_cam = [
        [
            rotation[i][0] * grot[0][k] + rotation[i][1] * grot[1][k] + rotation[i][2] * grot[2][k]
            for k in range(3)
        ]
        for i in range(3)
    ]
    row_one = [
        (
            focal_x * inverse * axes_cam[0][k]
            - focal_x * cam_pos[0] * inverse * inverse * axes_cam[2][k]
        )
        * scales[k]
        for k in range(3)
    ]
    row_two = [
        (
            focal_y * inverse * axes_cam[1][k]
            - focal_y * cam_pos[1] * inverse * inverse * axes_cam[2][k]
        )
        * scales[k]
        for k in range(3)
    ]
    entry_a = row_one[0] * row_one[0] + row_one[1] * row_one[1] + row_one[2] * row_one[2] + 0.3
    entry_b = row_one[0] * row_two[0] + row_one[1] * row_two[1] + row_one[2] * row_two[2]
    entry_c = row_two[0] * row_two[0] + row_two[1] * row_two[1] + row_two[2] * row_two[2] + 0.3
    determinant = entry_a * entry_c - entry_b * entry_b
    opacity = jax.nn.sigmoid(gauss[10])
    distance = jnp.sqrt(cam_pos[0] * cam_pos[0] + cam_pos[1] * cam_pos[1] + cam_pos[2] * cam_pos[2])
    direction = [
        (rotation[0][j] * cam_pos[0] + rotation[1][j] * cam_pos[1] + rotation[2][j] * cam_pos[2])
        / distance
        for j in range(3)
    ]
    basis = sh_basis(direction[0], direction[1], direction[2])
    colors = []
    for channel in range(3):
        accum = 0.5 + basis[0] * gauss[11 + channel]
        for order in range(1, 16):
            accum = accum + basis[order] * gauss[11 + 3 * order + channel]
        colors.append(jnp.maximum(accum, 0.0))
    return jnp.stack(
        [
            screen_u,
            screen_w,
            entry_c / determinant,
            -entry_b / determinant,
            entry_a / determinant,
            opacity,
        ]
        + colors
    )


def expand(blocks, order):
    tiles_n, width = blocks.shape
    visible = blocks >= 0
    slots = jnp.maximum(blocks, 0)
    inner_product = jnp.arange(BLOCK_GAUSSIANS, dtype=jnp.int32)
    positions = (slots[:, :, None] * BLOCK_GAUSSIANS + inner_product).reshape(
        tiles_n, width * BLOCK_GAUSSIANS
    )
    visible = jnp.broadcast_to(visible[:, :, None], (tiles_n, width, BLOCK_GAUSSIANS)).reshape(
        tiles_n, width * BLOCK_GAUSSIANS
    )
    positions = jnp.take_along_axis(positions, order, axis=1)
    visible = jnp.take_along_axis(visible, order, axis=1)
    return (positions, visible)


def composite(fields, positions, visible, goal, first_tile):
    count, length = positions.shape
    pixels = goal.shape[-1]
    group = math.gcd(count, 4)
    steps_n = count // group
    pixel_ids = jnp.arange(pixels, dtype=jnp.int32)
    offset_x = (pixel_ids % 16).astype(jnp.float32) + 0.5
    offset_y = (pixel_ids // 16).astype(jnp.float32) + 0.5

    def step(carry, item):
        indices, alive, wanted, number = item
        tiles = first_tile + number * group + jnp.arange(group, dtype=jnp.int32)
        pix_x = (tiles % TX * 16).astype(jnp.float32)[:, None] + offset_x
        pix_y = (tiles // TX * 16).astype(jnp.float32)[:, None] + offset_y
        weights_mask = alive.astype(jnp.float32)

        def render(local_part):
            delta_x = pix_x[:, None, :] - local_part[0][:, :, None]
            delta_y = pix_y[:, None, :] - local_part[1][:, :, None]
            power = (
                -0.5
                * (
                    local_part[2][:, :, None] * delta_x * delta_x
                    + local_part[4][:, :, None] * delta_y * delta_y
                )
                - local_part[3][:, :, None] * delta_x * delta_y
            )
            alpha_value = (local_part[5] * weights_mask)[:, :, None] * jnp.exp(power)
            logs = jnp.log1p(-alpha_value)
            transmit_factor = jnp.exp(jnp.cumsum(logs, axis=1) - logs)
            return jnp.einsum(
                "dal,jda->djl",
                alpha_value * transmit_factor,
                local_part[6:9],
                precision=HIGHEST_PRECISE,
            )

        local_part = fields[:, indices]
        color, pullback = jax.vjp(render, local_part)
        local_grad = pullback((color - wanted) / pixels)[0]
        carry = carry.at[:, indices.reshape(-1)].add(local_grad.reshape(local_grad.shape[0], -1))
        return (carry, color)

    items = (
        positions.reshape(steps_n, group, length),
        visible.reshape(steps_n, group, length),
        goal.reshape(steps_n, group, 3, pixels),
        jnp.arange(steps_n, dtype=jnp.int32),
    )
    total, colors = lax.scan(step, jnp.zeros_like(fields), items)
    return (colors.reshape(count, 3, pixels), total)


def local(params, camera, targets, send_blocks, tile_blocks, tile_order):
    cells = lax.axis_size("cell")
    cell_index = lax.axis_index("cell")
    camera_row = camera[0]
    values_n = params.shape[0]
    owned_blocks = params.shape[1] // BLOCK_GAUSSIANS
    per_peer = send_blocks.shape[3]
    width = per_peer * BLOCK_GAUSSIANS
    picks = send_blocks[0, 0].reshape(-1)
    chosen = jnp.take(
        params.reshape(values_n, owned_blocks, BLOCK_GAUSSIANS), picks, axis=1
    ).reshape(values_n, cells * width)
    positions, visible = expand(tile_blocks[0], tile_order[0])
    first_tile = cell_index * tile_blocks.shape[1]
    received = lax.all_to_all(
        chosen.reshape(values_n, cells, width), "cell", split_axis=1, concat_axis=1, tiled=True
    ).reshape(values_n, cells * width)
    arrived, pullback = jax.vjp(lambda gathered: project(gathered, camera_row), received)
    picture, field_grad = composite(arrived, positions, visible, targets[0], first_tile)
    slot_grad = pullback(field_grad)[0]
    sent_grad = lax.all_to_all(
        slot_grad.reshape(values_n, cells, width), "cell", split_axis=1, concat_axis=1, tiled=True
    ).reshape(values_n, cells * width)
    per_block = jnp.transpose(
        sent_grad.reshape(values_n, cells * per_peer, BLOCK_GAUSSIANS), (1, 0, 2)
    )
    summed = jax.ops.segment_sum(per_block, picks, num_segments=owned_blocks)
    summed = jnp.transpose(summed, (1, 0, 2)).reshape(values_n, owned_blocks * BLOCK_GAUSSIANS)
    total = lax.psum(summed, "view")
    return (picture[None], total)


def solution(mesh):
    return jax.shard_map(
        local,
        mesh=mesh,
        in_specs=(
            P(None, "cell"),
            P("view", None),
            P("view", "cell", None, None),
            P("view", "cell", None, None),
            P("view", "cell", None),
            P("view", "cell", None),
        ),
        out_specs=(P("view", "cell", None, None), P(None, "cell")),
        check_vma=False,
    )
```

profile of v0, /device:TPU:0, one launch (start us, length us, event | category | flops | bytes accessed | tf_op | source)
XLA Modules:
  0.0 1059.9 jit_solution(7028042116414189610)
XLA Ops:
  8.6 3.9 copy.133
  12.7 2.9 gather_fusion.1
  17.3 3.2 copy.134
  20.5 5.2 all-to-all-start
  39.2 137.9 %gather_fusion.3 = pred[16384]{0:T(1024)(128)(4,1)S(1)} fusion(pred[32,512]{1,0:T(8,128)(4,1)S(1)} %reshape.6814, s32[16384]{0:T(1024)S(1)} %bitcast.267), kind=kCustom, calls=%fused_computation.3 | custom fusion | bytes 163840 | tf_op jit(solution)/shard_map/jit(take_along_axis)/gather | solution.py:153
  177.6 129.5 %gather_fusion.2 = s32[16384]{0:T(1024)S(1)} fusion(s32[32,512]{1,0:T(8,128)S(1)} %broadcast_add_fusion.4, s32[16384]{0:T(1024)S(1)} %bitcast.268), kind=kCustom, calls=%fused_computation.2 | custom fusion | bytes 262144 | tf_op jit(solution)/shard_map/jit(take_along_axis)/gather | solution.py:152
  313.6 2.7 fusion.154
  331.4 563.3 %while.15 = (s32[]{:T(128)}, f32[9,4096]{0,1:T(8,128)}, f32[8,4,3,256]{3,2,1,0:T(4,128)}, s32[8,4,512]{2,1,0:T(4,128)}, f32[9,4096]{0,1:T(8,128)}, /*index=5*/pr...) while((s32[]{:T(128)}, f32[9,4096]{0,1:T(8,128)}, ...), condition=%wide.region_13.14_spmd.clone, body=%wide.region_1.13_spmd.clone.sunk | while | flops 240312416 | bytes 65026284 | solution.py:206
  346.5 7.0 gather_fusion
  358.4 4.7 fusion.184
  371.0 6.0 fusion.186
  377.0 9.6 fusion.187
  391.6 7.6 fusion.188
  400.8 12.2 %scatter_fusion = f32[9,4096]{0,1:T(8,128)S(1)} fusion(f32[9,4096]{0,1:T(8,128)S(1)} %copy-done.2, s32[2048]{0:T(1024)S(1)} %bitcast.313, f32[2048,9]{1,0:T(8,128)S(1)} %copy.228), kind=kCustom, calls=%fused_computation.4.clone.clone.1 | custom fusion | flops 18432 | bytes 229376 | tf_op jit(solution)/shard_map/while/body/eval_jaxpr/scatter-add | solution.py:197
  415.1 7.0 gather_fusion
  427.0 4.7 fusion.184
  439.6 6.0 fusion.186
  445.6 9.6 fusion.187
  460.2 7.6 fusion.188
  469.4 12.2 %scatter_fusion = f32[9,4096]{0,1:T(8,128)S(1)} fusion(f32[9,4096]{0,1:T(8,128)S(1)} %copy-done.2, s32[2048]{0:T(1024)S(1)} %bitcast.313, f32[2048,9]{1,0:T(8,128)S(1)} %copy.228), kind=kCustom, calls=%fused_computation.4.clone.clone.1 | custom fusion | flops 18432 | bytes 229376 | tf_op jit(solution)/shard_map/while/body/eval_jaxpr/scatter-add | solution.py:197
  483.7 7.0 gather_fusion
  495.6 4.7 fusion.184
  508.2 6.0 fusion.186
  514.3 9.6 fusion.187
  528.9 7.6 fusion.188
  538.0 12.2 %scatter_fusion = f32[9,4096]{0,1:T(8,128)S(1)} fusion(f32[9,4096]{0,1:T(8,128)S(1)} %copy-done.2, s32[2048]{0:T(1024)S(1)} %bitcast.313, f32[2048,9]{1,0:T(8,128)S(1)} %copy.228), kind=kCustom, calls=%fused_computation.4.clone.clone.1 | custom fusion | flops 18432 | bytes 229376 | tf_op jit(solution)/shard_map/while/body/eval_jaxpr/scatter-add | solution.py:197
  552.3 7.0 gather_fusion
  564.2 4.7 fusion.184
  576.8 6.0 fusion.186
  582.8 9.6 fusion.187
  597.4 7.6 fusion.188
  606.6 12.2 %scatter_fusion = f32[9,4096]{0,1:T(8,128)S(1)} fusion(f32[9,4096]{0,1:T(8,128)S(1)} %copy-done.2, s32[2048]{0:T(1024)S(1)} %bitcast.313, f32[2048,9]{1,0:T(8,128)S(1)} %copy.228), kind=kCustom, calls=%fused_computation.4.clone.clone.1 | custom fusion | flops 18432 | bytes 229376 | tf_op jit(solution)/shard_map/while/body/eval_jaxpr/scatter-add | solution.py:197
  620.9 7.0 gather_fusion
  632.8 4.7 fusion.184
  645.4 6.0 fusion.186
  651.4 9.6 fusion.187
  666.0 7.6 fusion.188
  675.2 12.2 %scatter_fusion = f32[9,4096]{0,1:T(8,128)S(1)} fusion(f32[9,4096]{0,1:T(8,128)S(1)} %copy-done.2, s32[2048]{0:T(1024)S(1)} %bitcast.313, f32[2048,9]{1,0:T(8,128)S(1)} %copy.228), kind=kCustom, calls=%fused_computation.4.clone.clone.1 | custom fusion | flops 18432 | bytes 229376 | tf_op jit(solution)/shard_map/while/body/eval_jaxpr/scatter-add | solution.py:197
  689.5 7.0 gather_fusion
  701.4 4.7 fusion.184
  714.1 6.0 fusion.186
  720.1 9.6 fusion.187
  734.7 7.6 fusion.188
  743.9 12.2 %scatter_fusion = f32[9,4096]{0,1:T(8,128)S(1)} fusion(f32[9,4096]{0,1:T(8,128)S(1)} %copy-done.2, s32[2048]{0:T(1024)S(1)} %bitcast.313, f32[2048,9]{1,0:T(8,128)S(1)} %copy.228), kind=kCustom, calls=%fused_computation.4.clone.clone.1 | custom fusion | flops 18432 | bytes 229376 | tf_op jit(solution)/shard_map/while/body/eval_jaxpr/scatter-add | solution.py:197
  758.1 7.0 gather_fusion
  770.0 4.7 fusion.184
  782.7 6.0 fusion.186
  788.7 9.6 fusion.187
  803.3 7.6 fusion.188
  812.5 12.2 %scatter_fusion = f32[9,4096]{0,1:T(8,128)S(1)} fusion(f32[9,4096]{0,1:T(8,128)S(1)} %copy-done.2, s32[2048]{0:T(1024)S(1)} %bitcast.313, f32[2048,9]{1,0:T(8,128)S(1)} %copy.228), kind=kCustom, calls=%fused_computation.4.clone.clone.1 | custom fusion | flops 18432 | bytes 229376 | tf_op jit(solution)/shard_map/while/body/eval_jaxpr/scatter-add | solution.py:197
  826.7 7.0 gather_fusion
  838.7 4.7 fusion.184
  851.3 6.0 fusion.186
  857.3 9.6 fusion.187
  871.9 7.6 fusion.188
  881.1 12.2 %scatter_fusion = f32[9,4096]{0,1:T(8,128)S(1)} fusion(f32[9,4096]{0,1:T(8,128)S(1)} %copy-done.2, s32[2048]{0:T(1024)S(1)} %bitcast.313, f32[2048,9]{1,0:T(8,128)S(1)} %copy.228), kind=kCustom, calls=%fused_computation.4.clone.clone.1 | custom fusion | flops 18432 | bytes 229376 | tf_op jit(solution)/shard_map/while/body/eval_jaxpr/scatter-add | solution.py:197
  910.2 3.9 broadcast_multiply_fusion.10
  916.1 3.4 fusion.80
  921.7 4.2 all-to-all-start.1
  926.1 15.2 %all-to-all-done.1 = f32[59,8,512]{2,0,1:T(8,128)S(1)} async-done(((f32[59,8,512]{2,0,1:T(8,128)}), f32[59,8,512]{2,0,1:T(8,128)S(1)}, u32[]{:S(2)}, u32[]{:S(2)}) %all-to-all-start.1) | async-done | bytes 966688 | tf_op jit(solution)/shard_map/all_to_all | solution.py:230
  944.5 15.5 %scatter_fusion.1 = f32[256,59,32]{1,2,0:T(8,128)} fusion(f32[256,59,32]{1,2,0:T(8,128)} %broadcast_in_dim.76, s32[128]{0:T(128)S(1)} %reshape.6864, f32[128,59,32]{1,2,0:T(8,128)S(1)} %bitcast.272), kind=kCustom, calls=%fused_computation.5 | custom fusion | flops 241664 | bytes 2900480 | tf_op jit(solution)/shard_map/scatter-add | solution.py:236
  960.0 3.8 copy.152
  965.4 84.2 %all-reduce.78.cloned.1.call-done = f32[59,8192]{1,0:T(8,128)} async-done(((f32[59,8192]{1,0:T(8,128)}), f32[59,8192]{1,0:T(8,128)}) %all-reduce.78.cloned.1.call-update) | async-done | bytes 1933328 | tf_op jit(solution)/shard_map/psum | solution.py:238
  1049.6 3.1 copy.244
  (961 shorter events, 213.1 us)
Async XLA Ops:
  17.3 8.4 copy-start.119
  17.3 8.5 copy-start.120
  17.3 9.8 copy-start.52
  20.5 289.3 %all-to-all-start = ((f32[59,8,512]{2,0,1:T(8,128)}), f32[59,8,512]{2,0,1:T(8,128)S(1)}, u32[]{:S(2)}, u32[]{:S(2)}) async-start(f32[59,8,512]{2,0,1:T(8,128)} %copy.134), calls=%async_computation | async-start | bytes 2097152 | tf_op jit(solution)/shard_map/all_to_all | solution.py:224
  177.6 129.5 %copy-start.117 = (f32[1,32,3,256]{3,1,2,0:T(8,128)S(1)}, f32[1,32,3,256]{3,1,2,0:T(8,128)}, u32[]{:S(2)}) copy-start(f32[1,32,3,256]{3,1,2,0:T(8,128)} %param.10) | copy-start | bytes 294916
  310.7 9.8 copy-start.53
  310.7 9.8 copy-start.55
  310.7 9.8 copy-start.57
  310.7 9.8 copy-start.59
  310.7 15.4 %copy-start.28 = (f32[1,8,512]{2,0,1:T(1,128)}, f32[1,8,512]{2,0,1:T(1,128)S(1)}, u32[]{:S(2)}) copy-start(f32[1,8,512]{2,0,1:T(1,128)S(1)} %get-tuple-element.415) | copy-start | bytes 49156
  312.3 10.5 copy-start.14
  313.6 9.1 copy-start.12
  313.6 12.6 %copy-start.50 = (f32[1,8,512]{2,0,1:T(1,128)}, f32[1,8,512]{2,0,1:T(1,128)S(1)}, u32[]{:S(2)}) copy-start(f32[1,8,512]{2,0,1:T(1,128)S(1)} %get-tuple-element.416) | copy-start | bytes 49156
  320.4 5.9 copy-start.77
  320.4 5.9 copy-start.79
  320.4 5.9 copy-start.81
  320.4 5.9 copy-start.83
  320.4 5.9 copy-start.85
  320.4 5.9 copy-start.87
  320.4 5.9 copy-start.89
  320.4 5.9 copy-start.91
  320.4 5.9 copy-start.93
  391.6 7.7 copy-start.31
  460.2 7.7 copy-start.31
  528.9 7.7 copy-start.31
  597.4 7.7 copy-start.31
  666.0 7.7 copy-start.31
  734.7 7.7 copy-start.31
  803.3 7.7 copy-start.31
  871.9 7.7 copy-start.31
  894.8 12.6 %copy-start.40 = (f32[1,4096]{1,0:T(1,128)S(1)}, f32[1,4096]{1,0:T(1,128)}, u32[]{:S(2)}) copy-start(f32[1,4096]{1,0:T(1,128)} %get-tuple-element.302) | copy-start | bytes 49156
  894.8 13.4 %copy-start.33 = (f32[1,4096]{1,0:T(1,128)S(1)}, f32[1,4096]{1,0:T(1,128)}, u32[]{:S(2)}) copy-start(f32[1,4096]{1,0:T(1,128)} %copy-done.32) | copy-start | bytes 49156
  894.8 13.4 %copy-start.35 = (f32[1,4096]{1,0:T(1,128)S(1)}, f32[1,4096]{1,0:T(1,128)}, u32[]{:S(2)}) copy-start(f32[1,4096]{1,0:T(1,128)} %copy-done.34) | copy-start | bytes 49156
  894.8 13.4 %copy-start.37 = (f32[1,4096]{1,0:T(1,128)S(1)}, f32[1,4096]{1,0:T(1,128)}, u32[]{:S(2)}) copy-start(f32[1,4096]{1,0:T(1,128)} %copy-done.36) | copy-start | bytes 49156
  894.8 13.4 %copy-start.39 = (f32[1,4096]{1,0:T(1,128)S(1)}, f32[1,4096]{1,0:T(1,128)}, u32[]{:S(2)}) copy-start(f32[1,4096]{1,0:T(1,128)} %copy-done.38) | copy-start | bytes 49156
  894.8 13.4 %copy-start.45 = (f32[1,4096]{1,0:T(1,128)S(1)}, f32[1,4096]{1,0:T(1,128)}, u32[]{:S(2)}) copy-start(f32[1,4096]{1,0:T(1,128)} %copy-done.44) | copy-start | bytes 49156
  894.8 13.4 %copy-start.47 = (f32[1,4096]{1,0:T(1,128)S(1)}, f32[1,4096]{1,0:T(1,128)}, u32[]{:S(2)}) copy-start(f32[1,4096]{1,0:T(1,128)} %copy-done.46) | copy-start | bytes 49156
  894.9 13.4 %copy-start.49 = (f32[1,4096]{1,0:T(1,128)S(1)}, f32[1,4096]{1,0:T(1,128)}, u32[]{:S(2)}) copy-start(f32[1,4096]{1,0:T(1,128)} %copy-done.48) | copy-start | bytes 49156
  897.1 12.8 %copy-start.41 = (f32[1,4096]{1,0:T(1,128)S(1)}, f32[1,4096]{1,0:T(1,128)}, u32[]{:S(2)}) copy-start(f32[1,4096]{1,0:T(1,128)} %get-tuple-element.321) | copy-start | bytes 49156
  897.1 12.8 %copy-start.42 = (f32[1,4096]{1,0:T(1,128)S(1)}, f32[1,4096]{1,0:T(1,128)}, u32[]{:S(2)}) copy-start(f32[1,4096]{1,0:T(1,128)} %get-tuple-element.327) | copy-start | bytes 49156
  897.1 12.8 %copy-start.43 = (f32[1,4096]{1,0:T(1,128)S(1)}, f32[1,4096]{1,0:T(1,128)}, u32[]{:S(2)}) copy-start(f32[1,4096]{1,0:T(1,128)} %get-tuple-element.333) | copy-start | bytes 49156
  897.2 12.8 %copy-start.51 = (f32[1,8,512]{2,0,1:T(1,128)S(1)}, f32[1,8,512]{2,0,1:T(1,128)}, u32[]{:S(2)}) copy-start(f32[1,8,512]{2,0,1:T(1,128)} %copy-done.50) | copy-start | bytes 49156
  897.2 12.8 %copy-start.70 = (f32[1,8,512]{2,0,1:T(1,128)S(1)}, f32[1,8,512]{2,0,1:T(1,128)}, u32[]{:S(2)}) copy-start(f32[1,8,512]{2,0,1:T(1,128)} %copy-done.69) | copy-start | bytes 49156
  897.2 12.8 %copy-start.72 = (f32[1,8,512]{2,0,1:T(1,128)S(1)}, f32[1,8,512]{2,0,1:T(1,128)}, u32[]{:S(2)}) copy-start(f32[1,8,512]{2,0,1:T(1,128)} %copy-done.71) | copy-start | bytes 49156
  897.2 12.8 %copy-start.74 = (f32[1,8,512]{2,0,1:T(1,128)S(1)}, f32[1,8,512]{2,0,1:T(1,128)}, u32[]{:S(2)}) copy-start(f32[1,8,512]{2,0,1:T(1,128)} %copy-done.73) | copy-start | bytes 49156
  897.2 12.8 %copy-start.76 = (f32[1,8,512]{2,0,1:T(1,128)S(1)}, f32[1,8,512]{2,0,1:T(1,128)}, u32[]{:S(2)}) copy-start(f32[1,8,512]{2,0,1:T(1,128)} %copy-done.75) | copy-start | bytes 49156
  897.2 12.8 %copy-start.78 = (f32[1,8,512]{2,0,1:T(1,128)S(1)}, f32[1,8,512]{2,0,1:T(1,128)}, u32[]{:S(2)}) copy-start(f32[1,8,512]{2,0,1:T(1,128)} %copy-done.77) | copy-start | bytes 49156
  897.2 12.8 %copy-start.80 = (f32[1,8,512]{2,0,1:T(1,128)S(1)}, f32[1,8,512]{2,0,1:T(1,128)}, u32[]{:S(2)}) copy-start(f32[1,8,512]{2,0,1:T(1,128)} %copy-done.79) | copy-start | bytes 49156
  897.2 12.8 %copy-start.82 = (f32[1,8,512]{2,0,1:T(1,128)S(1)}, f32[1,8,512]{2,0,1:T(1,128)}, u32[]{:S(2)}) copy-start(f32[1,8,512]{2,0,1:T(1,128)} %copy-done.81) | copy-start | bytes 49156
  897.2 12.8 %copy-start.84 = (f32[1,8,512]{2,0,1:T(1,128)S(1)}, f32[1,8,512]{2,0,1:T(1,128)}, u32[]{:S(2)}) copy-start(f32[1,8,512]{2,0,1:T(1,128)} %copy-done.83) | copy-start | bytes 49156
  897.2 12.8 %copy-start.86 = (f32[1,8,512]{2,0,1:T(1,128)S(1)}, f32[1,8,512]{2,0,1:T(1,128)}, u32[]{:S(2)}) copy-start(f32[1,8,512]{2,0,1:T(1,128)} %copy-done.85) | copy-start | bytes 49156
  897.3 12.8 %copy-start.88 = (f32[1,8,512]{2,0,1:T(1,128)S(1)}, f32[1,8,512]{2,0,1:T(1,128)}, u32[]{:S(2)}) copy-start(f32[1,8,512]{2,0,1:T(1,128)} %copy-done.87) | copy-start | bytes 49156
  897.3 12.8 %copy-start.90 = (f32[1,8,512]{2,0,1:T(1,128)S(1)}, f32[1,8,512]{2,0,1:T(1,128)}, u32[]{:S(2)}) copy-start(f32[1,8,512]{2,0,1:T(1,128)} %copy-done.89) | copy-start | bytes 49156
  897.3 12.8 %copy-start.92 = (f32[1,8,512]{2,0,1:T(1,128)S(1)}, f32[1,8,512]{2,0,1:T(1,128)}, u32[]{:S(2)}) copy-start(f32[1,8,512]{2,0,1:T(1,128)} %copy-done.91) | copy-start | bytes 49156
  897.3 12.8 %copy-start.94 = (f32[1,8,512]{2,0,1:T(1,128)S(1)}, f32[1,8,512]{2,0,1:T(1,128)}, u32[]{:S(2)}) copy-start(f32[1,8,512]{2,0,1:T(1,128)} %copy-done.93) | copy-start | bytes 49156
  898.4 9.9 copy-start.100
  898.4 11.7 %copy-start.96 = (f32[1,8,512]{2,0,1:T(1,128)S(1)}, f32[1,8,512]{2,0,1:T(1,128)}, u32[]{:S(2)}) copy-start(f32[1,8,512]{2,0,1:T(1,128)} %copy-done.95) | copy-start | bytes 49156
  898.4 11.7 %copy-start.98 = (f32[1,8,512]{2,0,1:T(1,128)S(1)}, f32[1,8,512]{2,0,1:T(1,128)}, u32[]{:S(2)}) copy-start(f32[1,8,512]{2,0,1:T(1,128)} %copy-done.97) | copy-start | bytes 49156
  898.4 11.7 %copy-start.101 = (f32[1,4096]{1,0:T(1,128)S(1)}, f32[1,4096]{1,0:T(1,128)}, u32[]{:S(2)}) copy-start(f32[1,4096]{1,0:T(1,128)} %get-tuple-element.297) | copy-start | bytes 49156
  899.4 10.8 %copy-start.102 = (f32[1,4096]{1,0:T(1,128)S(1)}, f32[1,4096]{1,0:T(1,128)}, u32[]{:S(2)}) copy-start(f32[1,4096]{1,0:T(1,128)} %get-tuple-element.300) | copy-start | bytes 49156
  900.4 9.8 copy-start.103
  900.4 9.8 copy-start.105
  921.7 19.6 %all-to-all-start.1 = ((f32[59,8,512]{2,0,1:T(8,128)}), f32[59,8,512]{2,0,1:T(8,128)S(1)}, u32[]{:S(2)}, u32[]{:S(2)}) async-start(f32[59,8,512]{2,0,1:T(8,128)} %copy.150), calls=%async_computation.1 | async-start | bytes 2097152 | tf_op jit(solution)/shard_map/all_to_all | solution.py:230
  925.9 123.6 %all-reduce.78.cloned.1.call-start = ((), (), s32[]{:S(2)}) async-start(), calls=%async_computation.2 | async-start | bytes 4194304 | tf_op jit(solution)/shard_map/psum | solution.py:238
  (186 other events, 448.9 us)
Sparse Core Ops, SparseCore 0:
  964.0 85.5 all-reduce.77
where the time goes:
time: 1070 us; the launch traced here: 1060 us
  local copies, waits for them, and re-layouts  444 us (41%)
  other arithmetic  374 us (35%)
  waiting for transfers between devices  99.4 us (9%)
  matrix products  82.1 us (8%)
  between operations  27.9 us (3%)
  loops' own time  23 us (2%)
    gather x2, local copies, waits for them, and re-layouts, expand(): visible = jnp.take_along_axis(visible, order, axis=1)  138 us
    another operation x48, other arithmetic  134 us
    gather x2, local copies, waits for them, and re-layouts, expand(): positions = jnp.take_along_axis(positions, order, axis=1)  129 us
    scatter-add x8, other arithmetic, step(): carry.at[:, indices.reshape(-1)]  97.8 us
    psum x1, waiting for transfers between devices, local(): total = lax.psum(summed, 'view')  84.2 us
    dot_general x24, matrix products, render(): jnp.einsum('dal,jda->djl', alpha_value * transmit_factor, local_part[6:9]...  82.1 us
    reduce_sum x8, other arithmetic, render(): local_part[3][:, :, None] * delta_x * delta_y  60.7 us
    gather x16, local copies, waits for them, and re-layouts, step(): local_part = fields[:, indices]  59 us
  transfers between devices with their start and end apart: 3, of which 2 were waited for; matrix products, arithmetic and copies ran while one was open for 26% of the time, Pallas kernels for 0%

commit v1 on v0

--- a/solution.py
+++ b/solution.py
@@ -25,6 +25,16 @@
     1.445305721320277,
     -0.5900435899266435,
 ]
+
+
+def table_choose(mine_x):
+    devs = lax.axis_size("view")
+    n_now = mine_x
+    for d in [k0 for k0 in (1, 2, 4, 8, 16) if k0 < devs]:
+        n_now = n_now + lax.ppermute(
+            n_now, axis_name="view", perm=tuple(((rr, rr ^ d) for rr in range(devs)))
+        )
+    return n_now
 
 
 def quat_matrix(qw, qx, qy, qz):
@@ -235,7 +245,7 @@
     )
     summed = jax.ops.segment_sum(per_block, picks, num_segments=owned_blocks)
     summed = jnp.transpose(summed, (1, 0, 2)).reshape(values_n, owned_blocks * BLOCK_GAUSSIANS)
-    total = lax.psum(summed, "view")
+    total = table_choose(summed)
     return (picture[None], total)
 
 

time: 1070 us -> 1110 us (1.037)
  waiting for transfers between devices: 99.4 us -> 144 us
  between operations: 27.9 us -> 15 us
    ppermute x0 -> x2, waiting for transfers between devices: none -> 129 us  [table_choose(): lax.ppermute(n_now, axis_name='view', perm=tuple(((rr, rr ^ d) for rr in...]
    psum x1 -> x0, waiting for transfers between devices: 84.2 us -> none  [local(): total = lax.psum(summed, 'view')]
  transfers between devices with their start and end apart: 3 -> 4, of which waited for: 2 -> 3; matrix products, arithmetic and copies ran while one was open for 26% -> 25% of each run, Pallas kernels for 0% -> 0%
where the time goes in v1:
time: 1110 us; the launch traced here: 1090 us
  local copies, waits for them, and re-layouts  440 us (40%)
  other arithmetic  375 us (34%)
  waiting for transfers between devices  144 us (13%)
  matrix products  81.8 us (7%)
  loops' own time  23.3 us (2%)
  between operations  15 us (1%)
  starting transfers between devices  14.6 us (1%)
    gather x2, local copies, waits for them, and re-layouts, expand(): visible = jnp.take_along_axis(visible, order, axis=1)  138 us
    another operation x48, other arithmetic  134 us
    gather x2, local copies, waits for them, and re-layouts, expand(): positions = jnp.take_along_axis(positions, order, axis=1)  129 us
    ppermute x2, waiting for transfers between devices, table_choose(): lax.ppermute(n_now, axis_name='view', perm=tuple(((rr, rr ^ d) for rr in...  129 us
    scatter-add x8, other arithmetic, step(): carry.at[:, indices.reshape(-1)]  97.8 us
    dot_general x24, matrix products, render(): jnp.einsum('dal,jda->djl', alpha_value * transmit_factor, local_part[6:9]...  81.8 us
    reduce_sum x8, other arithmetic, render(): local_part[3][:, :, None] * delta_x * delta_y  60.7 us
    gather x16, local copies, waits for them, and re-layouts, step(): local_part = fields[:, indices]  59 us
  transfers between devices with their start and end apart: 4, of which 3 were waited for; matrix products, arithmetic and copies ran while one was open for 25% of the time, Pallas kernels for 0%

profile of v1, /device:TPU:0, one launch (start us, length us, event | category | flops | bytes accessed | tf_op | source)
XLA Modules:
  0.0 1093.7 jit_solution(8785311185021395666)
XLA Ops:
  2.1 3.9 copy.137
  6.2 2.9 gather_fusion.1
  10.8 3.2 copy.138
  14.0 5.2 all-to-all-start
  33.2 137.9 %gather_fusion.3 = pred[16384]{0:T(1024)(128)(4,1)S(1)} fusion(pred[32,512]{1,0:T(8,128)(4,1)S(1)} %reshape.6814, s32[16384]{0:T(1024)S(1)} %bitcast.267), kind=kCustom, calls=%fused_computation.3 | custom fusion | bytes 163840 | tf_op jit(solution)/shard_map/jit(take_along_axis)/gather | solution.py:163
  171.6 129.5 %gather_fusion.2 = s32[16384]{0:T(1024)S(1)} fusion(s32[32,512]{1,0:T(8,128)S(1)} %broadcast_add_fusion.4, s32[16384]{0:T(1024)S(1)} %bitcast.268), kind=kCustom, calls=%fused_computation.2 | custom fusion | bytes 262144 | tf_op jit(solution)/shard_map/jit(take_along_axis)/gather | solution.py:162
  325.3 563.9 %while.15 = (s32[]{:T(128)}, f32[9,4096]{0,1:T(8,128)}, f32[8,4,3,256]{3,2,1,0:T(4,128)}, s32[8,4,512]{2,1,0:T(4,128)}, f32[9,4096]{0,1:T(8,128)}, /*index=5*/pr...) while((s32[]{:T(128)}, f32[9,4096]{0,1:T(8,128)}, ...), condition=%wide.region_13.14_spmd.clone, body=%wide.region_1.13_spmd.clone.sunk | while | flops 240312416 | bytes 65026284 | solution.py:216
  340.4 7.0 gather_fusion
  352.4 4.7 fusion.184
  365.1 6.0 fusion.186
  371.1 9.6 fusion.187
  385.6 7.6 fusion.188
  394.8 12.2 %scatter_fusion = f32[9,4096]{0,1:T(8,128)S(1)} fusion(f32[9,4096]{0,1:T(8,128)S(1)} %copy-done.2, s32[2048]{0:T(1024)S(1)} %bitcast.313, f32[2048,9]{1,0:T(8,128)S(1)} %copy.233), kind=kCustom, calls=%fused_computation.4.clone.clone.1 | custom fusion | flops 18432 | bytes 229376 | tf_op jit(solution)/shard_map/while/body/eval_jaxpr/scatter-add | solution.py:207
  409.1 7.0 gather_fusion
  421.1 4.7 fusion.184
  433.8 6.0 fusion.186
  439.7 9.6 fusion.187
  454.3 7.6 fusion.188
  463.5 12.2 %scatter_fusion = f32[9,4096]{0,1:T(8,128)S(1)} fusion(f32[9,4096]{0,1:T(8,128)S(1)} %copy-done.2, s32[2048]{0:T(1024)S(1)} %bitcast.313, f32[2048,9]{1,0:T(8,128)S(1)} %copy.233), kind=kCustom, calls=%fused_computation.4.clone.clone.1 | custom fusion | flops 18432 | bytes 229376 | tf_op jit(solution)/shard_map/while/body/eval_jaxpr/scatter-add | solution.py:207
  477.8 7.0 gather_fusion
  489.8 4.7 fusion.184
  502.4 6.0 fusion.186
  508.4 9.6 fusion.187
  523.0 7.6 fusion.188
  532.2 12.2 %scatter_fusion = f32[9,4096]{0,1:T(8,128)S(1)} fusion(f32[9,4096]{0,1:T(8,128)S(1)} %copy-done.2, s32[2048]{0:T(1024)S(1)} %bitcast.313, f32[2048,9]{1,0:T(8,128)S(1)} %copy.233), kind=kCustom, calls=%fused_computation.4.clone.clone.1 | custom fusion | flops 18432 | bytes 229376 | tf_op jit(solution)/shard_map/while/body/eval_jaxpr/scatter-add | solution.py:207
  546.5 7.0 gather_fusion
  558.5 4.7 fusion.184
  571.1 6.0 fusion.186
  577.1 9.6 fusion.187
  591.7 7.6 fusion.188
  600.9 12.2 %scatter_fusion = f32[9,4096]{0,1:T(8,128)S(1)} fusion(f32[9,4096]{0,1:T(8,128)S(1)} %copy-done.2, s32[2048]{0:T(1024)S(1)} %bitcast.313, f32[2048,9]{1,0:T(8,128)S(1)} %copy.233), kind=kCustom, calls=%fused_computation.4.clone.clone.1 | custom fusion | flops 18432 | bytes 229376 | tf_op jit(solution)/shard_map/while/body/eval_jaxpr/scatter-add | solution.py:207
  615.2 7.0 gather_fusion
  627.2 4.7 fusion.184
  639.8 6.0 fusion.186
  645.8 9.6 fusion.187
  660.4 7.6 fusion.188
  669.6 12.2 %scatter_fusion = f32[9,4096]{0,1:T(8,128)S(1)} fusion(f32[9,4096]{0,1:T(8,128)S(1)} %copy-done.2, s32[2048]{0:T(1024)S(1)} %bitcast.313, f32[2048,9]{1,0:T(8,128)S(1)} %copy.233), kind=kCustom, calls=%fused_computation.4.clone.clone.1 | custom fusion | flops 18432 | bytes 229376 | tf_op jit(solution)/shard_map/while/body/eval_jaxpr/scatter-add | solution.py:207
  683.8 7.0 gather_fusion
  695.9 4.7 fusion.184
  708.5 6.0 fusion.186
  714.5 9.6 fusion.187
  729.1 7.6 fusion.188
  738.3 12.2 %scatter_fusion = f32[9,4096]{0,1:T(8,128)S(1)} fusion(f32[9,4096]{0,1:T(8,128)S(1)} %copy-done.2, s32[2048]{0:T(1024)S(1)} %bitcast.313, f32[2048,9]{1,0:T(8,128)S(1)} %copy.233), kind=kCustom, calls=%fused_computation.4.clone.clone.1 | custom fusion | flops 18432 | bytes 229376 | tf_op jit(solution)/shard_map/while/body/eval_jaxpr/scatter-add | solution.py:207
  752.6 7.0 gather_fusion
  764.6 4.7 fusion.184
  777.2 6.0 fusion.186
  783.2 9.6 fusion.187
  797.8 7.6 fusion.188
  807.0 12.2 %scatter_fusion = f32[9,4096]{0,1:T(8,128)S(1)} fusion(f32[9,4096]{0,1:T(8,128)S(1)} %copy-done.2, s32[2048]{0:T(1024)S(1)} %bitcast.313, f32[2048,9]{1,0:T(8,128)S(1)} %copy.233), kind=kCustom, calls=%fused_computation.4.clone.clone.1 | custom fusion | flops 18432 | bytes 229376 | tf_op jit(solution)/shard_map/while/body/eval_jaxpr/scatter-add | solution.py:207
  821.2 7.0 gather_fusion
  833.3 4.7 fusion.184
  845.9 6.0 fusion.186
  851.9 9.6 fusion.187
  866.5 7.6 fusion.188
  875.7 12.2 %scatter_fusion = f32[9,4096]{0,1:T(8,128)S(1)} fusion(f32[9,4096]{0,1:T(8,128)S(1)} %copy-done.2, s32[2048]{0:T(1024)S(1)} %bitcast.313, f32[2048,9]{1,0:T(8,128)S(1)} %copy.233), kind=kCustom, calls=%fused_computation.4.clone.clone.1 | custom fusion | flops 18432 | bytes 229376 | tf_op jit(solution)/shard_map/while/body/eval_jaxpr/scatter-add | solution.py:207
  904.4 3.8 broadcast_multiply_fusion.10
  910.1 3.4 fusion.80
  915.8 4.2 all-to-all-start.1
  920.1 15.3 %all-to-all-done.1 = f32[59,8,512]{2,0,1:T(8,128)S(1)} async-done(((f32[59,8,512]{2,0,1:T(8,128)}), f32[59,8,512]{2,0,1:T(8,128)S(1)}, u32[]{:S(2)}, u32[]{:S(2)}) %all-to-all-start.1) | async-done | bytes 966688 | tf_op jit(solution)/shard_map/all_to_all | solution.py:240
  938.6 15.5 %scatter_fusion.1 = f32[256,59,32]{1,2,0:T(8,128)} fusion(f32[256,59,32]{1,2,0:T(8,128)} %broadcast_in_dim.76, s32[128]{0:T(128)S(1)} %reshape.6864, f32[128,59,32]{1,2,0:T(8,128)S(1)} %bitcast.272), kind=kCustom, calls=%fused_computation.5 | custom fusion | flops 241664 | bytes 2900480 | tf_op jit(solution)/shard_map/scatter-add | solution.py:246
  954.1 2.9 copy.157
  958.6 43.1 %collective-permute-done = f32[59,8192]{1,0:T(8,128)S(1)} collective-permute-done((f32[59,8192]{1,0:T(8,128)S(1)}, f32[59,8192]{1,0:T(8,128)S(1)}, u32[]{:S(2)}, u32[]{:S(2)}) %collective-permute-start) | collective-permute-done | bytes 1933344 | tf_op jit(solution)/shard_map/ppermute | solution.py:34
  1002.0 3.6 collective-permute-start.1
  1006.2 85.5 %collective-permute-done.1 = f32[59,8192]{1,0:T(8,128)S(1)} collective-permute-done((f32[59,8192]{1,0:T(8,128)S(1)}, f32[59,8192]{1,0:T(8,128)S(1)}, u32[]{:S(2)}, u32[]{:S(2)}) %collective-permute-start.1) | collective-permute-done | bytes 1933344 | tf_op jit(solution)/shard_map/ppermute | solution.py:34
  (963 shorter events, 218.4 us)
Async XLA Ops:
  10.8 8.4 copy-start.119
  10.8 8.5 copy-start.120
  10.8 9.8 copy-start.52
  14.0 289.8 %all-to-all-start = ((f32[59,8,512]{2,0,1:T(8,128)}), f32[59,8,512]{2,0,1:T(8,128)S(1)}, u32[]{:S(2)}, u32[]{:S(2)}) async-start(f32[59,8,512]{2,0,1:T(8,128)} %copy.138), calls=%async_computation | async-start | bytes 2097152 | tf_op jit(solution)/shard_map/all_to_all | solution.py:234
  171.6 129.5 %copy-start.117 = (f32[1,32,3,256]{3,1,2,0:T(8,128)S(1)}, f32[1,32,3,256]{3,1,2,0:T(8,128)}, u32[]{:S(2)}) copy-start(f32[1,32,3,256]{3,1,2,0:T(8,128)} %param.10) | copy-start | bytes 294916
  304.7 9.7 copy-start.53
  304.7 9.7 copy-start.55
  304.7 9.7 copy-start.57
  304.8 9.7 copy-start.59
  304.8 15.3 %copy-start.28 = (f32[1,8,512]{2,0,1:T(1,128)}, f32[1,8,512]{2,0,1:T(1,128)S(1)}, u32[]{:S(2)}) copy-start(f32[1,8,512]{2,0,1:T(1,128)S(1)} %get-tuple-element.415) | copy-start | bytes 49156
  306.2 10.5 copy-start.14
  307.6 9.1 copy-start.12
  307.6 12.5 %copy-start.50 = (f32[1,8,512]{2,0,1:T(1,128)}, f32[1,8,512]{2,0,1:T(1,128)S(1)}, u32[]{:S(2)}) copy-start(f32[1,8,512]{2,0,1:T(1,128)S(1)} %get-tuple-element.416) | copy-start | bytes 49156
  314.3 5.9 copy-start.77
  314.3 5.9 copy-start.79
  314.3 5.9 copy-start.81
  314.3 5.9 copy-start.83
  314.3 5.9 copy-start.85
  314.3 5.9 copy-start.87
  314.3 5.9 copy-start.89
  385.6 7.7 copy-start.31
  454.3 7.7 copy-start.31
  523.0 7.7 copy-start.31
  591.7 7.7 copy-start.31
  660.4 7.7 copy-start.31
  729.1 7.7 copy-start.31
  797.8 7.7 copy-start.31
  866.5 7.7 copy-start.31
  889.4 12.2 %copy-start.40 = (f32[1,4096]{1,0:T(1,128)S(1)}, f32[1,4096]{1,0:T(1,128)}, u32[]{:S(2)}) copy-start(f32[1,4096]{1,0:T(1,128)} %get-tuple-element.302) | copy-start | bytes 49156
  889.4 13.1 %copy-start.33 = (f32[1,4096]{1,0:T(1,128)S(1)}, f32[1,4096]{1,0:T(1,128)}, u32[]{:S(2)}) copy-start(f32[1,4096]{1,0:T(1,128)} %copy-done.32) | copy-start | bytes 49156
  889.4 13.1 %copy-start.35 = (f32[1,4096]{1,0:T(1,128)S(1)}, f32[1,4096]{1,0:T(1,128)}, u32[]{:S(2)}) copy-start(f32[1,4096]{1,0:T(1,128)} %copy-done.34) | copy-start | bytes 49156
  889.4 13.1 %copy-start.37 = (f32[1,4096]{1,0:T(1,128)S(1)}, f32[1,4096]{1,0:T(1,128)}, u32[]{:S(2)}) copy-start(f32[1,4096]{1,0:T(1,128)} %copy-done.36) | copy-start | bytes 49156
  889.4 13.1 %copy-start.39 = (f32[1,4096]{1,0:T(1,128)S(1)}, f32[1,4096]{1,0:T(1,128)}, u32[]{:S(2)}) copy-start(f32[1,4096]{1,0:T(1,128)} %copy-done.38) | copy-start | bytes 49156
  889.4 13.1 %copy-start.45 = (f32[1,4096]{1,0:T(1,128)S(1)}, f32[1,4096]{1,0:T(1,128)}, u32[]{:S(2)}) copy-start(f32[1,4096]{1,0:T(1,128)} %copy-done.44) | copy-start | bytes 49156
  889.4 13.1 %copy-start.47 = (f32[1,4096]{1,0:T(1,128)S(1)}, f32[1,4096]{1,0:T(1,128)}, u32[]{:S(2)}) copy-start(f32[1,4096]{1,0:T(1,128)} %copy-done.46) | copy-start | bytes 49156
  889.4 13.1 %copy-start.49 = (f32[1,4096]{1,0:T(1,128)S(1)}, f32[1,4096]{1,0:T(1,128)}, u32[]{:S(2)}) copy-start(f32[1,4096]{1,0:T(1,128)} %copy-done.48) | copy-start | bytes 49156
  891.7 12.5 %copy-start.41 = (f32[1,4096]{1,0:T(1,128)S(1)}, f32[1,4096]{1,0:T(1,128)}, u32[]{:S(2)}) copy-start(f32[1,4096]{1,0:T(1,128)} %get-tuple-element.321) | copy-start | bytes 49156
  891.7 12.5 %copy-start.42 = (f32[1,4096]{1,0:T(1,128)S(1)}, f32[1,4096]{1,0:T(1,128)}, u32[]{:S(2)}) copy-start(f32[1,4096]{1,0:T(1,128)} %get-tuple-element.327) | copy-start | bytes 49156
  891.7 12.5 %copy-start.43 = (f32[1,4096]{1,0:T(1,128)S(1)}, f32[1,4096]{1,0:T(1,128)}, u32[]{:S(2)}) copy-start(f32[1,4096]{1,0:T(1,128)} %get-tuple-element.333) | copy-start | bytes 49156
  891.7 12.5 %copy-start.51 = (f32[1,8,512]{2,0,1:T(1,128)S(1)}, f32[1,8,512]{2,0,1:T(1,128)}, u32[]{:S(2)}) copy-start(f32[1,8,512]{2,0,1:T(1,128)} %copy-done.50) | copy-start | bytes 49156
  891.7 12.5 %copy-start.70 = (f32[1,8,512]{2,0,1:T(1,128)S(1)}, f32[1,8,512]{2,0,1:T(1,128)}, u32[]{:S(2)}) copy-start(f32[1,8,512]{2,0,1:T(1,128)} %copy-done.69) | copy-start | bytes 49156
  891.7 12.5 %copy-start.72 = (f32[1,8,512]{2,0,1:T(1,128)S(1)}, f32[1,8,512]{2,0,1:T(1,128)}, u32[]{:S(2)}) copy-start(f32[1,8,512]{2,0,1:T(1,128)} %copy-done.71) | copy-start | bytes 49156
  891.8 12.5 %copy-start.74 = (f32[1,8,512]{2,0,1:T(1,128)S(1)}, f32[1,8,512]{2,0,1:T(1,128)}, u32[]{:S(2)}) copy-start(f32[1,8,512]{2,0,1:T(1,128)} %copy-done.73) | copy-start | bytes 49156
  891.8 12.5 %copy-start.76 = (f32[1,8,512]{2,0,1:T(1,128)S(1)}, f32[1,8,512]{2,0,1:T(1,128)}, u32[]{:S(2)}) copy-start(f32[1,8,512]{2,0,1:T(1,128)} %copy-done.75) | copy-start | bytes 49156
  891.8 12.5 %copy-start.78 = (f32[1,8,512]{2,0,1:T(1,128)S(1)}, f32[1,8,512]{2,0,1:T(1,128)}, u32[]{:S(2)}) copy-start(f32[1,8,512]{2,0,1:T(1,128)} %copy-done.77) | copy-start | bytes 49156
  891.8 12.5 %copy-start.80 = (f32[1,8,512]{2,0,1:T(1,128)S(1)}, f32[1,8,512]{2,0,1:T(1,128)}, u32[]{:S(2)}) copy-start(f32[1,8,512]{2,0,1:T(1,128)} %copy-done.79) | copy-start | bytes 49156
  891.8 12.5 %copy-start.82 = (f32[1,8,512]{2,0,1:T(1,128)S(1)}, f32[1,8,512]{2,0,1:T(1,128)}, u32[]{:S(2)}) copy-start(f32[1,8,512]{2,0,1:T(1,128)} %copy-done.81) | copy-start | bytes 49156
  891.8 12.5 %copy-start.84 = (f32[1,8,512]{2,0,1:T(1,128)S(1)}, f32[1,8,512]{2,0,1:T(1,128)}, u32[]{:S(2)}) copy-start(f32[1,8,512]{2,0,1:T(1,128)} %copy-done.83) | copy-start | bytes 49156
  891.8 12.5 %copy-start.86 = (f32[1,8,512]{2,0,1:T(1,128)S(1)}, f32[1,8,512]{2,0,1:T(1,128)}, u32[]{:S(2)}) copy-start(f32[1,8,512]{2,0,1:T(1,128)} %copy-done.85) | copy-start | bytes 49156
  891.8 12.5 %copy-start.88 = (f32[1,8,512]{2,0,1:T(1,128)S(1)}, f32[1,8,512]{2,0,1:T(1,128)}, u32[]{:S(2)}) copy-start(f32[1,8,512]{2,0,1:T(1,128)} %copy-done.87) | copy-start | bytes 49156
  891.8 12.5 %copy-start.90 = (f32[1,8,512]{2,0,1:T(1,128)S(1)}, f32[1,8,512]{2,0,1:T(1,128)}, u32[]{:S(2)}) copy-start(f32[1,8,512]{2,0,1:T(1,128)} %copy-done.89) | copy-start | bytes 49156
  891.8 12.5 %copy-start.92 = (f32[1,8,512]{2,0,1:T(1,128)S(1)}, f32[1,8,512]{2,0,1:T(1,128)}, u32[]{:S(2)}) copy-start(f32[1,8,512]{2,0,1:T(1,128)} %copy-done.91) | copy-start | bytes 49156
  891.9 12.5 %copy-start.94 = (f32[1,8,512]{2,0,1:T(1,128)S(1)}, f32[1,8,512]{2,0,1:T(1,128)}, u32[]{:S(2)}) copy-start(f32[1,8,512]{2,0,1:T(1,128)} %copy-done.93) | copy-start | bytes 49156
  892.9 9.5 copy-start.100
  893.0 11.4 %copy-start.96 = (f32[1,8,512]{2,0,1:T(1,128)S(1)}, f32[1,8,512]{2,0,1:T(1,128)}, u32[]{:S(2)}) copy-start(f32[1,8,512]{2,0,1:T(1,128)} %copy-done.95) | copy-start | bytes 49156
  893.0 11.4 %copy-start.98 = (f32[1,8,512]{2,0,1:T(1,128)S(1)}, f32[1,8,512]{2,0,1:T(1,128)}, u32[]{:S(2)}) copy-start(f32[1,8,512]{2,0,1:T(1,128)} %copy-done.97) | copy-start | bytes 49156
  893.0 11.4 %copy-start.101 = (f32[1,4096]{1,0:T(1,128)S(1)}, f32[1,4096]{1,0:T(1,128)}, u32[]{:S(2)}) copy-start(f32[1,4096]{1,0:T(1,128)} %get-tuple-element.297) | copy-start | bytes 49156
  893.9 10.5 copy-start.102
  894.9 9.5 copy-start.103
  894.9 9.5 copy-start.105
  915.8 19.6 %all-to-all-start.1 = ((f32[59,8,512]{2,0,1:T(8,128)}), f32[59,8,512]{2,0,1:T(8,128)S(1)}, u32[]{:S(2)}, u32[]{:S(2)}) async-start(f32[59,8,512]{2,0,1:T(8,128)} %copy.154), calls=%async_computation.1 | async-start | bytes 2097152 | tf_op jit(solution)/shard_map/all_to_all | solution.py:240
  957.0 48.6 %copy-start.116 = (f32[8,4,3,256]{3,2,1,0:T(4,128)S(1)}, f32[8,4,3,256]{3,2,1,0:T(4,128)}, u32[]{:S(2)}) copy-start(f32[8,4,3,256]{3,2,1,0:T(4,128)} %get-tuple-element.143) | copy-start | bytes 294916
  957.0 44.7 %collective-permute-start = (f32[59,8192]{1,0:T(8,128)S(1)}, f32[59,8192]{1,0:T(8,128)S(1)}, u32[]{:S(2)}, u32[]{:S(2)}) collective-permute-start(f32[59,8192]{1,0:T(8,128)S(1)} %copy.157), channel_id=1, source_target_pairs={{0,8},{8,0},{16,24},{24,16},{1,9},{9,1},{17,25},{25,17},{2,10},{10... | collective-permute-start | bytes 5799944 | tf_op jit(solution)/shard_map/ppermute | solution.py:34
  1002.0 89.7 %collective-permute-start.1 = (f32[59,8192]{1,0:T(8,128)S(1)}, f32[59,8192]{1,0:T(8,128)S(1)}, u32[]{:S(2)}, u32[]{:S(2)}) collective-permute-start(f32[59,8192]{1,0:T(8,128)S(1)} %add.8886), channel_id=1, source_target_pairs={{0,16},{8,24},{16,0},{24,8},{1,17},{9,25},{17,1},{25,9},{2,18},{10... | collective-permute-start | bytes 5799944 | tf_op jit(solution)/shard_map/ppermute | solution.py:34
  (187 other events, 461.5 us)
